TPU v7x, 512 devices: a whole 4x4x16 slice. The times are simulated.
512 devices in a mesh: pix: 64 (over z, y), train: 8 (over x, core).
Axes of the slice: x: 4, y: 4, z: 16, core: 2. Of those that a mesh axis runs over, the one named last changes fastest.
Arguments:
- raw_frames: bfloat16 [24, 352, 16384], P('train', None, 'pix'), may hold values from 60 to 160
- gain_section: int32 [24, 352, 16384], P('train', None, 'pix'), may hold values from 0 to 2
- dark_offset: bfloat16 [3, 352, 16384], P(None, None, 'pix'), may hold values from 0 to 40
- rel_gain: float32 [3, 16384], P(None, 'pix'), may hold values from 0.5 to 8
- cycle_label: int32 [16384, 1], P('pix'), may hold values from 0 to 191; in each aligned block of 256 rows (0 to 255, 256 to 511, ...) at most 2 rows name the same one
- cycle_slot: int32 [192], replicated, may hold values from 0 to 191, each once
Outputs:
- two_time: float32 [192, 352, 352], P('pix', 'train')
Inputs may be any that keep to these rules, and one draw needn't show every extreme that they name: `cycle_label`: among the pixels of one index of pix no cycle holds more than 2 pixels; every cycle holds some pixel. `cycle_slot`: A permutation of the cycles.
All inputs are finite; a program needn't handle non-finite values.
Results may differ from a plain program's by a relative error of at most 0.0003.
Values sent between devices are 32-bit elements; how exact they have to be, the bound alone decides.
A program may use at most 64 MiB of HBM per device.

v0:
```python
import jax
import jax.numpy as jnp
from jax import lax
from jax.sharding import PartitionSpec as P

CYCLE_DEV = 3


def on_device(raw_frames, gain_section, dark_offset, rel_gain, cycle_label, cycle_slot):
    trains, pulses, pixels = raw_frames.shape
    owners = lax.axis_size("pix")
    cycle_count = CYCLE_DEV * owners
    slot_depth = 2 * pixels // cycle_count
    section_zero = gain_section == 0
    section_one = gain_section == 1
    offset = jnp.where(
        section_zero, dark_offset[0], jnp.where(section_one, dark_offset[1], dark_offset[2])
    ).astype(jnp.float32)
    factor = jnp.where(section_zero, rel_gain[0], jnp.where(section_one, rel_gain[1], rel_gain[2]))
    intensity = (raw_frames.astype(jnp.float32) - offset) * factor
    pixel_rows = jnp.transpose(intensity, (2, 0, 1)).reshape(pixels, trains * pulses)
    labels = cycle_label[:, 0]
    member = labels[:, None] == jnp.arange(cycle_count, dtype=jnp.int32)[None, :]
    slot_of = jnp.sum(jnp.where(member, cycle_slot[None, :], 0), axis=1)
    running = jnp.cumsum(member.astype(jnp.int32), axis=0)
    within_cycle = jnp.sum(jnp.where(member, running, 0), axis=1) - 1
    cycle_counts = jnp.sum(member.astype(jnp.int32), axis=0)
    slot_member = cycle_slot[:, None] == jnp.arange(cycle_count, dtype=jnp.int32)[None, :]
    slot_counts = jnp.sum(jnp.where(slot_member, cycle_counts[:, None], 0), axis=0)
    position = slot_of * slot_depth + within_cycle
    buffer = (
        jnp.zeros((cycle_count * slot_depth, trains * pulses), jnp.float32)
        .at[position]
        .set(pixel_rows)
    )
    buffer = buffer.reshape(owners, CYCLE_DEV, slot_depth, trains * pulses)
    cycle_tally = slot_counts.astype(jnp.float32).reshape(owners, CYCLE_DEV, 1)
    slot_data = lax.all_to_all(buffer, "pix", split_axis=0, concat_axis=2, tiled=True)
    numbers = lax.all_to_all(cycle_tally, "pix", split_axis=0, concat_axis=2, tiled=True)
    item_count = slot_data.shape[1]
    blocks = slot_data.reshape(item_count, slot_data.shape[2], trains, pulses)
    gram_sum = jnp.einsum("kstf,kstg->kfg", blocks, blocks, precision=lax.Precision.HIGHEST)
    frame_means = jnp.sum(blocks, axis=(1, 2))
    gram_sum, frame_means, number = (
        gram_sum,
        frame_means,
        jnp.sum(numbers.reshape(item_count, numbers.shape[2]), axis=1),
    )
    groups = lax.axis_size("train")
    all_trains = trains * groups
    row_band = pulses // groups
    row_start = lax.axis_index("train") * row_band
    gram_whole, means_whole = lax.psum((gram_sum, frame_means), "train")
    gram_rows = lax.dynamic_slice_in_dim(gram_whole, row_start, row_band, 1)
    means_rows = lax.dynamic_slice_in_dim(means_whole, row_start, row_band, 1)
    cycle_scale = all_trains * number
    return (
        cycle_scale[:, None, None] * gram_rows / (means_rows[:, :, None] * means_whole[:, None, :])
    )


def solution(mesh):
    placed = (
        P("train", None, "pix"),
        P("train", None, "pix"),
        P(None, None, "pix"),
        P(None, "pix"),
        P("pix", None),
        P(),
    )
    return jax.shard_map(
        on_device, mesh=mesh, in_specs=placed, out_specs=P("pix", "train", None), check_vma=False
    )
```

profile of v0, /device:TPU:8, one launch (start us, length us, event | category | flops | bytes accessed | tf_op | source)
XLA Modules:
  0.0 208.9 jit_solution(14207055044721804327)
XLA Ops:
  6.5 0.0 copy-start.1
  6.5 0.0 copy-start
  6.5 0.0 copy-start.2
  6.5 0.0 all-reduce.2.cloned.1.call-start
  6.5 0.9 fusion.12
  7.4 0.8 copy.22
  8.2 0.2 fusion.7
  8.5 0.2 copy.23
  8.7 0.9 convert_reduce_fusion
  9.5 0.0 copy-done.1
  9.6 0.0 copy-done
  9.6 0.0 copy-done.2
  9.6 0.4 select_multiply_fusion
  10.0 0.4 copy.24
  10.4 1.9 scatter_custom_fusion
  12.2 1.1 reshape.82
  13.3 104.6 %all_to_all.24 = f32[64,3,2,1056]{3,2,1,0:T(2,128)S(1)} all-to-all(f32[64,3,2,1056]{3,2,1,0:T(2,128)S(1)} %reshape.82), channel_id=1, replica_groups=mesh['pix'=64,'train'=8] {'pix'}, dimensions={0} | all-to-all | bytes 3244032 | tf_op jit(solution)/shard_map/all_to_all | solution.py:38
  117.9 0.6 copy.25
  118.5 3.4 %reshape.83 = f32[3,128,3,352]{3,2,1,0:T(4,128)} reshape(f32[1,3,64,2,1056]{4,3,2,1,0:T(2,128)S(1)} %copy.25) | data formatting | bytes 3244032 | tf_op jit(solution)/shard_map/reshape | solution.py:41
  121.9 6.9 %fusion.2 = f32[3,352,352]{2,1,0:T(8,128)} fusion(f32[3,128,3,352]{3,2,1,0:T(4,128)} %reshape.83), kind=kOutput, calls=%fused_computation.3 | convolution fusion | flops 1712848896 | bytes 3108864 | tf_op jit(solution)/shard_map/kstf,kstg->kfg/dot_general | solution.py:42
  128.7 0.0 copy-start.3
  128.7 0.0 all-reduce.2.cloned.1.call-update
  128.8 0.7 copy-done.3
  129.4 0.1 select_reduce_fusion.1
  129.6 0.8 convert_element_type.29
  130.3 6.0 %all-to-all-start = ((f32[64,3,1]{1,2,0:T(1,128)}), f32[64,3,1]{1,2,0:T(1,128)S(1)}, u32[]{:S(2)}, u32[]{:S(2)}) async-start(f32[64,3,1]{1,2,0:T(1,128)} %bitcast.1), calls=%async_computation | async-start | bytes 65536 | tf_op jit(solution)/shard_map/all_to_all | solution.py:39
  136.3 13.7 %all-to-all-done = f32[64,3,1]{1,2,0:T(1,128)S(1)} async-done(((f32[64,3,1]{1,2,0:T(1,128)}), f32[64,3,1]{1,2,0:T(1,128)S(1)}, u32[]{:S(2)}, u32[]{:S(2)}) %all-to-all-start) | async-done | bytes 800 | tf_op jit(solution)/shard_map/all_to_all | solution.py:39
  150.0 0.1 reduce_sum.63
  150.1 0.4 bitcast_reduce_fusion
  150.5 0.1 reduce_sum.67
  150.6 12.8 %psum.15 = f32[3,352]{1,0:T(4,128)S(1)} all-reduce(f32[3,352]{1,0:T(4,128)S(1)} %reduce_sum.68), channel_id=1, replica_groups=mesh['pix'=64,'train'=8] {'train'}, use_global_device_ids=true, to_apply=%region_11.12 | all-reduce | flops 1056 | bytes 8448 | tf_op jit(solution)/shard_map/psum | solution.py:53
  163.5 0.1 constant_dynamic-slice_fusion
  163.5 36.8 %all-reduce.2.cloned.1.call-done = f32[3,352,352]{2,1,0:T(8,128)} async-done(((f32[3,352,352]{2,1,0:T(8,128)}), f32[3,352,352]{2,1,0:T(8,128)}) %all-reduce.2.cloned.1.call-update) | async-done | bytes 1486864 | tf_op jit(solution)/shard_map/psum | solution.py:53
  200.3 1.7 multiply_divide_fusion
  (11 shorter events, 0.2 us)
Async XLA Ops:
  6.5 3.0 %copy-start.1 = (bf16[3,352,256]{2,1,0:T(8,128)(2,1)S(1)}, bf16[3,352,256]{2,1,0:T(8,128)(2,1)}, u32[]{:S(2)}) copy-start(bf16[3,352,256]{2,1,0:T(8,128)(2,1)} %param.8) | copy-start | bytes 1622020
  6.5 3.1 %copy-start = (s32[3,352,256]{2,1,0:T(8,128)S(1)}, s32[3,352,256]{2,1,0:T(8,128)}, u32[]{:S(2)}) copy-start(s32[3,352,256]{2,1,0:T(8,128)} %param.7) | copy-start | bytes 3244036
  6.5 3.1 %copy-start.2 = (bf16[3,352,256]{2,1,0:T(8,128)(2,1)S(1)}, bf16[3,352,256]{2,1,0:T(8,128)(2,1)}, u32[]{:S(2)}) copy-start(bf16[3,352,256]{2,1,0:T(8,128)(2,1)} %param.6) | copy-start | bytes 1622020
  6.5 193.8 %all-reduce.2.cloned.1.call-start = ((), (), s32[]{:S(2)}) async-start(), calls=%async_computation.2 | async-start | bytes 3244032 | tf_op jit(solution)/shard_map/psum | solution.py:53
  128.7 0.7 copy-start.3
  130.3 19.7 %all-to-all-start = ((f32[64,3,1]{1,2,0:T(1,128)}), f32[64,3,1]{1,2,0:T(1,128)S(1)}, u32[]{:S(2)}, u32[]{:S(2)}) async-start(f32[64,3,1]{1,2,0:T(1,128)} %bitcast.1), calls=%async_computation | async-start | bytes 65536 | tf_op jit(solution)/shard_map/all_to_all | solution.py:39
Sparse Core Ops, SparseCore 0:
  128.9 71.4 all-reduce.1
where the time goes:
time: 209 us
  blocking collectives  117 us (56%)
  waiting for transfers between devices  50.5 us (24%)
  between operations  13.5 us (6%)
  local copies, waits for them, and re-layouts  10.7 us (5%)
  matrix products  6.85 us (3%)
  starting transfers between devices  5.95 us (3%)
  other arithmetic  3.88 us (2%)
    all_to_all x1, blocking collectives, on_device(): lax.all_to_all(buffer, 'pix', split_axis=0, concat_axis=2, tiled=True)  105 us
    psum x1, waiting for transfers between devices, on_device(): gram_whole, means_whole = lax.psum((gram_sum, frame_means), 'train')  36.8 us
    all_to_all x1, waiting for transfers between devices, on_device(): lax.all_to_all(cycle_tally, 'pix', split_axis=0, concat_axis=2, tiled=True)  13.7 us
    psum x1, blocking collectives, on_device(): gram_whole, means_whole = lax.psum((gram_sum, frame_means), 'train')  12.8 us
    dot_general x1, matrix products, on_device(): jnp.einsum('kstf,kstg->kfg', blocks, blocks, precision=lax.Precision.HIGH...  6.85 us
    all_to_all x1, starting transfers between devices, on_device(): lax.all_to_all(cycle_tally, 'pix', split_axis=0, concat_axis=2, tiled=True)  5.95 us
  transfers between devices with their start and end apart: 2, of which 2 were waited for; matrix products, arithmetic and copies ran while one was open for 1% of the time, Pallas kernels for 0%

commit v1 on v0

v1 whole, which is shorter than its diff:
```python
import jax
import jax.numpy as jnp
from jax import lax
from jax.sharding import PartitionSpec as P

CYCLE_DEV = 3
DEPTH = 2
BAND_PAD = 48


def slot_rows(raw_frames, gain_section, dark_offset, rel_gain, labels, slots, cycle_slot, bands):
    trains, pulses, pixels = raw_frames.shape
    section_zero = gain_section == 0
    section_one = gain_section == 1
    offset = jnp.where(
        section_zero, dark_offset[0], jnp.where(section_one, dark_offset[1], dark_offset[2])
    ).astype(jnp.float32)
    factor = jnp.where(section_zero, rel_gain[0], jnp.where(section_one, rel_gain[1], rel_gain[2]))
    intensity = (raw_frames.astype(jnp.float32) - offset) * factor
    band = pulses // bands
    grouped = intensity.reshape(trains, bands, band, pixels)
    ones = jnp.ones((trains, bands, 1, pixels), jnp.float32)
    zeros = jnp.zeros((trains, bands, BAND_PAD - band - 1, pixels), jnp.float32)
    grouped = jnp.concatenate([grouped, ones, zeros], axis=2).reshape(-1, pixels)
    cycle_count = cycle_slot.shape[0]
    member = labels[None, :] == jnp.arange(cycle_count, dtype=jnp.int32)[:, None]
    slot_of = jnp.sum(jnp.where(member, cycle_slot[:, None], 0), axis=0)
    index = jnp.arange(pixels, dtype=jnp.int32)
    earlier = (labels[:, None] == labels[None, :]) & (index[:, None] < index[None, :])
    within = jnp.sum(earlier.astype(jnp.int32), axis=0)
    position = slot_of * DEPTH + within
    chosen = (slots[:, None] == position[None, :]).astype(jnp.float32)
    return lax.dot_general(
        chosen, grouped, (((1,), (1,)), ((), ())), precision=lax.Precision.HIGHEST
    )


def normalise(total, band, bands):
    scale = total[:, band, band]
    rows_mean = total[:, :band, band]
    spread = total.reshape(total.shape[0], BAND_PAD, bands, BAND_PAD)[:, :, :, :band]
    spread = spread.reshape(total.shape[0], BAND_PAD, bands * band)
    return (
        scale[:, None, None]
        * spread[:, :band]
        / (rows_mean[:, :, None] * spread[:, band : band + 1, :])
    )


def on_device(raw_frames, gain_section, dark_offset, rel_gain, cycle_label, cycle_slot):
    trains, pulses, pixels = raw_frames.shape
    owners = lax.axis_size("pix")
    bands = lax.axis_size("train")
    cycle_count = cycle_slot.shape[0]
    slots = jnp.arange(cycle_count * DEPTH, dtype=jnp.int32)
    rows = slot_rows(
        raw_frames, gain_section, dark_offset, rel_gain, cycle_label[:, 0], slots, cycle_slot, bands
    )
    rows = rows.reshape(owners, CYCLE_DEV, DEPTH, -1)
    rows = lax.all_to_all(rows, "pix", split_axis=0, concat_axis=0, tiled=True)
    blocks = rows.reshape(owners, CYCLE_DEV, DEPTH, trains, bands * BAND_PAD)
    gram = jnp.einsum("okstf,okstg->kfg", blocks, blocks, precision=lax.Precision.HIGHEST)
    gram = gram.reshape(CYCLE_DEV, bands, BAND_PAD, bands * BAND_PAD)
    total = lax.psum_scatter(gram, "train", scatter_dimension=1, tiled=True)[:, 0]
    return normalise(total, pulses // bands, bands)


def solution(mesh):
    placed = (
        P("train", None, "pix"),
        P("train", None, "pix"),
        P(None, None, "pix"),
        P(None, "pix"),
        P("pix", None),
        P(),
    )
    return jax.shard_map(
        on_device, mesh=mesh, in_specs=placed, out_specs=P("pix", "train", None), check_vma=False
    )
```

time: 209 us -> 174 us (0.83)
  waiting for transfers between devices: 50.5 us -> 32.5 us
  blocking collectives: 117 us -> 105 us
  starting transfers between devices: 5.95 us -> 0.01 us
    psum x1 -> x0, waiting for transfers between devices: 36.8 us -> none  [on_device(): gram_whole, means_whole = lax.psum((gram_sum, frame_means), 'train')]
    reduce_scatter x0 -> x1, waiting for transfers between devices: none -> 32.4 us  [on_device(): lax.psum_scatter(gram, 'train', scatter_dimension=1, tiled=True)[:, 0]]
    all_to_all x1 -> x0, waiting for transfers between devices: 13.7 us -> none  [on_device(): lax.all_to_all(cycle_tally, 'pix', split_axis=0, concat_axis=2, tiled=True)]
    psum x1 -> x0, blocking collectives: 12.8 us -> none  [on_device(): gram_whole, means_whole = lax.psum((gram_sum, frame_means), 'train')]
    all_to_all x1 -> x0, starting transfers between devices: 5.95 us -> none  [on_device(): lax.all_to_all(cycle_tally, 'pix', split_axis=0, concat_axis=2, tiled=True)]
    dot_general x1 -> x2, matrix products: 6.85 us -> 7.36 us  [the longest x1 6.3 us: on_device(): jnp.einsum('okstf,okstg->kfg', blocks, blocks, precision=lax.Precision.HI...]
    reshape x3 -> x4, local copies, waits for them, and re-layouts: 4.83 us -> 4.63 us  [the longest x1 2.98 us: on_device(): blocks = rows.reshape(owners, CYCLE_DEV, DEPTH, trains, bands * BAND_PAD)]
  transfers between devices with their start and end apart: 2 -> 1, of which waited for: 2 -> 1; matrix products, arithmetic and copies ran while one was open for 1% -> 0% of each run, Pallas kernels for 0% -> 0%
where the time goes in v1:
time: 174 us; the launch traced here: 173 us
  blocking collectives  105 us (60%)
  waiting for transfers between devices  32.5 us (19%)
  between operations  13.5 us (8%)
  local copies, waits for them, and re-layouts  11.2 us (6%)
  matrix products  7.36 us (4%)
  other arithmetic  4.14 us (2%)
    all_to_all x1, blocking collectives, on_device(): rows = lax.all_to_all(rows, 'pix', split_axis=0, concat_axis=0, tiled=True)  105 us
    reduce_scatter x1, waiting for transfers between devices, on_device(): lax.psum_scatter(gram, 'train', scatter_dimension=1, tiled=True)[:, 0]  32.4 us
    dot_general x1, matrix products, on_device(): jnp.einsum('okstf,okstg->kfg', blocks, blocks, precision=lax.Precision.HI...  6.3 us
  transfers between devices with their start and end apart: 1, of which 1 were waited for; matrix products, arithmetic and copies ran while one was open for 0% of the time, Pallas kernels for 0%

profile of v1, /device:TPU:8, one launch (start us, length us, event | category | flops | bytes accessed | tf_op | source)
XLA Modules:
  0.0 173.2 jit_solution(4739895183160292655)
XLA Ops:
  6.5 0.0 copy-start
  6.5 0.0 reduce-scatter.2.cloned.1.call-start
  6.5 0.1 pad.1.clone
  6.6 0.1 pad.2.clone
  6.7 0.9 convert_reduce_fusion
  7.6 0.8 select_reduce_fusion
  8.4 0.8 fusion.8
  9.2 1.1 slice_bitcast_fusion.2
  10.3 0.0 copy-done
  10.4 1.4 select_multiply_fusion
  11.8 0.1 reshape.46
  11.9 0.2 maximum_maximum_fusion
  12.1 1.1 fusion.2
  13.2 1.4 copy.25
  14.6 104.6 %all_to_all.5 = f32[64,3,2,1152]{3,2,1,0:T(2,128)S(1)} all-to-all(f32[64,3,2,1152]{3,2,1,0:T(2,128)S(1)} %copy.25), channel_id=1, replica_groups=mesh['pix'=64,'train'=8] {'pix'}, dimensions={0} | all-to-all | bytes 3538944 | tf_op jit(solution)/shard_map/all_to_all | solution.py:60
  119.2 3.0 %reshape.53 = f32[64,3,2,3,384]{4,3,2,1,0:T(4,128)} reshape(f32[64,3,2,1152]{3,2,1,0:T(2,128)S(1)} %all_to_all.5) | data formatting | bytes 3538944 | tf_op jit(solution)/shard_map/reshape | solution.py:61
  122.1 6.3 %fusion = f32[3,384,384,1,1]{2,1,4,3,0:T(8,128)S(1)} fusion(f32[64,3,2,3,384]{4,3,2,1,0:T(4,128)} %reshape.53), kind=kOutput, calls=%fused_computation | convolution fusion | flops 2038431744 | bytes 3538944 | tf_op jit(solution)/shard_map/okstf,okstg->kfg/dot_general | solution.py:62
  128.4 1.3 copy.29
  129.8 0.0 reduce-scatter.2.cloned.1.call-update
  129.8 32.4 %reduce-scatter.2.cloned.1.call-done = f32[3,1,48,384]{3,2,0,1:T(8,128)} async-done(((f32[3,8,48,384]{3,2,0,1:T(8,128)}), f32[3,1,48,384]{3,2,0,1:T(8,128)}) %reduce-scatter.2.cloned.1.call-update) | async-done | bytes 221200 | tf_op jit(solution)/shard_map/reduce_scatter | solution.py:64
  162.2 0.9 slice_reduce_fusion.1
  163.1 1.0 slice_reduce_fusion
  164.2 1.2 reshape_squeeze.3
  165.4 0.2 reshape.50
  165.6 0.8 fusion.5
  (5 shorter events, 0.0 us)
Async XLA Ops:
  6.5 3.8 %copy-start = (s32[3,352,256]{2,1,0:T(8,128)S(1)}, s32[3,352,256]{2,1,0:T(8,128)}, u32[]{:S(2)}) copy-start(s32[3,352,256]{2,1,0:T(8,128)} %param.7) | copy-start | bytes 3244036
  6.5 155.7 %reduce-scatter.2.cloned.1.call-start = ((), (), s32[]{:S(2)}) async-start(), calls=%async_computation.2 | async-start | bytes 1990656 | tf_op jit(solution)/shard_map/reduce_scatter | solution.py:64
Sparse Core Ops, SparseCore 0:
  129.9 32.2 reduce-scatter.1

commit v2 on v1

--- a/solution.py
+++ b/solution.py
@@ -1,11 +1,234 @@
+import functools
+
 import jax
 import jax.numpy as jnp
 from jax import lax
+from jax.experimental import pallas as pl
+from jax.experimental.pallas import tpu as pltpu
 from jax.sharding import PartitionSpec as P
 
 CYCLE_DEV = 3
 DEPTH = 2
 BAND_PAD = 48
+LANES = 128
+TILES = 3
+BANDS = 8
+ROWS = 8
+Y = 4
+Z = 16
+HALF = Z // 2
+PEERS = Y * BANDS
+LAG = 3
+BLOCKS = [(b, j) for b in range(BANDS) for j in range(BAND_PAD * b // LANES, TILES)]
+PER_CYCLE = len(BLOCKS)
+PIECES = PER_CYCLE * CYCLE_DEV
+MESH = pl.DeviceIdType.MESH
+
+
+def kernel(
+    send, out, recv, gram, up_buf, dn_buf, full, fin,
+    own_sem, swap_send, swap_recv, up_send, dn_send, up_recv, dn_recv, fin_send, fin_recv,
+):
+    pix = lax.axis_index("pix")
+    t = lax.axis_index("train")
+    z, y = pix // Y, pix % Y
+    me = y * BANDS + t
+    turn = (z - t + Z) % Z
+    s = turn % HALF
+    far = jnp.where(turn < HALF, 1, 0)
+    near = 1 - far
+    above = {"pix": ((z + 1) % Z) * Y + y, "train": t}
+    below = {"pix": ((z + Z - 1) % Z) * Y + y, "train": t}
+
+    def peer(d):
+        return {"pix": z * Y + d // BANDS, "train": d % BANDS}
+
+    barrier = pltpu.get_barrier_semaphore()
+
+    @pl.loop(1, PEERS)
+    def _(i):
+        pl.semaphore_signal(barrier, inc=1, device_id=peer((me + i) % PEERS), device_id_type=MESH)
+
+    pl.semaphore_signal(barrier, inc=1, device_id=above, device_id_type=MESH)
+    pl.semaphore_signal(barrier, inc=1, device_id=below, device_id_type=MESH)
+    pl.semaphore_wait(barrier, PEERS + 1)
+
+    for m in range(CYCLE_DEV):
+
+        @pl.loop(1, PEERS)
+        def _(i):
+            d = (me + i) % PEERS
+            pltpu.make_async_remote_copy(
+                src_ref=send.at[m, d], dst_ref=recv.at[m, me],
+                send_sem=swap_send.at[m], recv_sem=swap_recv.at[m],
+                device_id=peer(d), device_id_type=MESH,
+            ).start()
+
+        pltpu.make_async_copy(send.at[m, me], recv.at[m, me], own_sem.at[m]).start()
+
+    @pl.loop(0, CYCLE_DEV)
+    def _(m):
+        pltpu.make_async_copy(send.at[m, me], recv.at[m, me], own_sem.at[m]).wait()
+        others = recv.at[m, pl.ds(0, PEERS - 1)]
+        pltpu.make_async_copy(others, others, swap_recv.at[m]).wait()
+        for h in range(2):
+            rows = recv[m, :, h].reshape(PEERS * ROWS, TILES * LANES)
+            head = rows.astype(jnp.bfloat16)
+            tail = (rows - head.astype(jnp.float32)).astype(jnp.bfloat16)
+            turned = rows.T
+            head_t = turned.astype(jnp.bfloat16)
+            tail_t = (turned - head_t.astype(jnp.float32)).astype(jnp.bfloat16)
+            for j in range(TILES):
+                bands = [b for b in range(BANDS) if BAND_PAD * b // LANES == j]
+                low, high = bands[0] * BAND_PAD, (bands[-1] + 1) * BAND_PAD
+                dot = functools.partial(jnp.dot, preferred_element_type=jnp.float32)
+                right, right_tail = head[:, j * LANES :], tail[:, j * LANES :]
+                part = (
+                    dot(head_t[low:high], right)
+                    + dot(head_t[low:high], right_tail)
+                    + dot(tail_t[low:high], right)
+                )
+                for b in bands:
+                    for jj in range(j, TILES):
+                        gram[h, m * PER_CYCLE + BLOCKS.index((b, jj))] = part[
+                            b * BAND_PAD - low : (b + 1) * BAND_PAD - low,
+                            (jj - j) * LANES : (jj - j + 1) * LANES,
+                        ]
+
+    def up_copy(p):
+        return pltpu.make_async_remote_copy(
+            src_ref=gram.at[far, p], dst_ref=up_buf.at[p], send_sem=up_send, recv_sem=up_recv.at[p],
+            device_id=above, device_id_type=MESH,
+        )
+
+    def dn_copy(p):
+        return pltpu.make_async_remote_copy(
+            src_ref=gram.at[near, p], dst_ref=dn_buf.at[p], send_sem=dn_send, recv_sem=dn_recv.at[p],
+            device_id=below, device_id_type=MESH,
+        )
+
+    def hand_out(m, b):
+        return pltpu.make_async_remote_copy(
+            src_ref=full.at[m, b], dst_ref=fin.at[m], send_sem=fin_send.at[m], recv_sem=fin_recv.at[m],
+            device_id={"pix": pix, "train": b}, device_id_type=MESH,
+        )
+
+    up_lag = s * LAG
+    dn_lag = jnp.where(s == 0, HALF * LAG, (HALF - 1 - s) * LAG)
+
+    @pl.loop(0, PIECES + HALF * LAG)
+    def _(step):
+        p = step - up_lag
+
+        @pl.when((p >= 0) & (p < PIECES))
+        def _():
+            @pl.when(s > 0)
+            def _():
+                up_copy(p).wait_recv()
+                gram[far, p] = gram[far, p] + up_buf[p]
+
+            up_copy(p).start()
+
+        q = step - dn_lag
+
+        @pl.when((q >= 0) & (q < PIECES))
+        def _():
+            @pl.when(s > 0)
+            def _():
+                @pl.when(s < HALF - 1)
+                def _():
+                    dn_copy(q).wait_recv()
+                    gram[near, q] = gram[near, q] + dn_buf[q]
+
+                dn_copy(q).start()
+
+            @pl.when(s == 0)
+            def _():
+                up_copy(q).wait_recv()
+                dn_copy(q).wait_recv()
+                gram[near, q] = gram[near, q] + (up_buf[q] + dn_buf[q])
+
+                @pl.when(q % PER_CYCLE == PER_CYCLE - 1)
+                def _():
+                    m = q // PER_CYCLE
+
+                    def block(b, j):
+                        return gram[near, m * PER_CYCLE + BLOCKS.index((b, j))]
+
+                    for b, j in BLOCKS:
+                        full[m, b, j] = block(b, j)
+                    first = jnp.concatenate(
+                        [
+                            jnp.concatenate([block(0, j), block(1, j), block(2, j)[:32]], 0).T
+                            for j in (1, 2)
+                        ],
+                        0,
+                    )
+                    for b in range(3, BANDS):
+                        full[m, b, 0] = first[b * BAND_PAD - LANES : (b + 1) * BAND_PAD - LANES]
+                    second = jnp.concatenate(
+                        [block(2, 2)[32:], block(3, 2), block(4, 2), block(5, 2)[:16]], 0
+                    ).T
+                    for b in range(6, BANDS):
+                        low = b * BAND_PAD - 2 * LANES
+                        full[m, b, 1] = second[low : low + BAND_PAD]
+
+                    @pl.loop(1, BANDS)
+                    def _(i):
+                        hand_out(m, (t + i) % BANDS).start()
+
+    @pl.loop(0, CYCLE_DEV)
+    def _(m):
+        @pl.when(s > 0)
+        def _():
+            hand_out(m, 0).wait_recv()
+            for j in range(TILES):
+                out[m, :, j * LANES : (j + 1) * LANES] = fin[m, j]
+
+        @pl.when(s == 0)
+        def _():
+            for j in range(TILES):
+                out[m, :, j * LANES : (j + 1) * LANES] = full[m, t, j]
+            sent = full.at[m, pl.ds(0, BANDS - 1)]
+            pltpu.make_async_copy(sent, sent, fin_send.at[m]).wait()
+
+        others = send.at[m, pl.ds(0, PEERS - 1)]
+        pltpu.make_async_copy(others, others, swap_send.at[m]).wait()
+
+    pltpu.make_async_copy(up_buf, up_buf, up_send).wait()
+
+    @pl.when(s > 0)
+    def _():
+        pltpu.make_async_copy(dn_buf, dn_buf, dn_send).wait()
+
+
+def summed_bands(send):
+    piece = (BAND_PAD, LANES)
+    return pl.pallas_call(
+        kernel,
+        out_shape=jax.ShapeDtypeStruct((CYCLE_DEV, BAND_PAD, TILES * LANES), jnp.float32),
+        in_specs=[pl.BlockSpec(memory_space=pltpu.VMEM)],
+        out_specs=pl.BlockSpec(memory_space=pltpu.VMEM),
+        scratch_shapes=[
+            pltpu.VMEM((CYCLE_DEV, PEERS, 2, ROWS, TILES * LANES), jnp.float32),
+            pltpu.VMEM((2, PIECES) + piece, jnp.float32),
+            pltpu.VMEM((PIECES,) + piece, jnp.float32),
+            pltpu.VMEM((PIECES,) + piece, jnp.float32),
+            pltpu.VMEM((CYCLE_DEV, BANDS, TILES) + piece, jnp.float32),
+            pltpu.VMEM((CYCLE_DEV, TILES) + piece, jnp.float32),
+            pltpu.SemaphoreType.DMA((CYCLE_DEV,)),
+            pltpu.SemaphoreType.DMA((CYCLE_DEV,)),
+            pltpu.SemaphoreType.DMA((CYCLE_DEV,)),
+            pltpu.SemaphoreType.DMA,
+            pltpu.SemaphoreType.DMA,
+            pltpu.SemaphoreType.DMA((PIECES,)),
+            pltpu.SemaphoreType.DMA((PIECES,)),
+            pltpu.SemaphoreType.DMA((CYCLE_DEV,)),
+            pltpu.SemaphoreType.DMA((CYCLE_DEV,)),
+        ],
+        compiler_params=pltpu.CompilerParams(collective_id=0, has_side_effects=True),
+        name="plane_gram",
+    )(send)
 
 
 def slot_rows(raw_frames, gain_section, dark_offset, rel_gain, labels, slots, cycle_slot, bands):
@@ -49,20 +272,18 @@
 
 def on_device(raw_frames, gain_section, dark_offset, rel_gain, cycle_label, cycle_slot):
     trains, pulses, pixels = raw_frames.shape
-    owners = lax.axis_size("pix")
-    bands = lax.axis_size("train")
-    cycle_count = cycle_slot.shape[0]
-    slots = jnp.arange(cycle_count * DEPTH, dtype=jnp.int32)
+    order = jnp.arange(CYCLE_DEV * Z * Y, dtype=jnp.int32)
+    m, rest = order // (PEERS * 2), order % (PEERS * 2)
+    peer, half = rest // 2, rest % 2
+    owner = (half * HALF + peer % BANDS) * Y + peer // BANDS
+    slots = (owner * CYCLE_DEV + m)[:, None] * DEPTH + jnp.arange(DEPTH, dtype=jnp.int32)[None, :]
     rows = slot_rows(
-        raw_frames, gain_section, dark_offset, rel_gain, cycle_label[:, 0], slots, cycle_slot, bands
-    )
-    rows = rows.reshape(owners, CYCLE_DEV, DEPTH, -1)
-    rows = lax.all_to_all(rows, "pix", split_axis=0, concat_axis=0, tiled=True)
-    blocks = rows.reshape(owners, CYCLE_DEV, DEPTH, trains, bands * BAND_PAD)
-    gram = jnp.einsum("okstf,okstg->kfg", blocks, blocks, precision=lax.Precision.HIGHEST)
-    gram = gram.reshape(CYCLE_DEV, bands, BAND_PAD, bands * BAND_PAD)
-    total = lax.psum_scatter(gram, "train", scatter_dimension=1, tiled=True)[:, 0]
-    return normalise(total, pulses // bands, bands)
+        raw_frames, gain_section, dark_offset, rel_gain, cycle_label[:, 0], slots.reshape(-1),
+        cycle_slot, BANDS,
+    )
+    rows = rows.reshape(CYCLE_DEV, PEERS, 2, DEPTH * trains, TILES * LANES)
+    rows = jnp.pad(rows, ((0, 0), (0, 0), (0, 0), (0, ROWS - DEPTH * trains), (0, 0)))
+    return normalise(summed_bands(rows), pulses // BANDS, BANDS)
 
 
 def solution(mesh):

time: 174 us -> 143 us (0.82)
  the two profiles are of different devices: /device:TPU:8 before, /device:TPU:5 now
where the time goes in v2:
time: 143 us; the launch traced here: 142 us
  Pallas kernels  127 us (89%)
  local copies, waits for them, and re-layouts  9.03 us (6%)
  other arithmetic  4.23 us (3%)
  matrix products  2.27 us (2%)
    pallas_call x1, Pallas kernels, summed_bands(): pl.pallas_call(kernel, out_shape=jax.ShapeDtypeStruct((CYCLE_DEV, BAND_PA...  127 us

profile of v2, /device:TPU:5, one launch (start us, length us, event | category | flops | bytes accessed | tf_op | source)
XLA Modules:
  0.0 142.3 jit_solution(1388485919105579115)
XLA Ops:
  0.0 0.0 copy-start
  0.0 0.1 pad.6.clone
  0.1 0.1 pad.7.clone
  0.2 0.9 convert_reduce_fusion
  1.0 0.8 select_reduce_fusion
  1.9 0.8 fusion.13
  2.7 0.1 iota_add_fusion
  2.8 0.1 add.100
  2.9 1.1 slice_bitcast_fusion.2
  4.1 0.0 copy-done
  4.1 1.4 select_multiply_fusion
  5.5 0.1 reshape.117
  5.6 0.2 maximum_maximum_fusion
  5.8 2.3 %fusion = f32[384,1152]{1,0:T(8,128)} fusion(f32[1152,256]{1,0:T(8,128)S(1)} %bitcast.19, s32[256]{0:T(256)S(1)} %multiply_add_fusion, s32[384]{0:T(512)S(1)} %add.100), kind=kOutput, calls=%fused_computation.2 | convolution fusion | flops 1359052800 | bytes 2951680 | tf_op jit(solution)/shard_map/dot_general | solution.py:256
  8.1 1.7 %reshape.119 = f32[3,32,2,6,384]{4,3,2,1,0:T(8,128)S(1)} reshape(f32[384,1152]{1,0:T(8,128)} %fusion) | data formatting | bytes 3538944 | tf_op jit(solution)/shard_map/reshape | solution.py:284
  9.8 1.6 %pad.4.send = f32[3,32,2,8,384]{4,3,2,1,0:T(8,128)} pad(f32[3,32,2,6,384]{4,3,2,1,0:T(8,128)S(1)} %reshape.119, f32[]{:T(128)} %constant.82.clone.1), padding=0_0x0_0x0_0x0_2x0_0 | pad | bytes 4128772 | tf_op jit(solution)/shard_map/jit(_pad)/pad | solution.py:285
  11.5 126.7 %plane_gram.1 = f32[3,48,384]{2,1,0:T(8,128)} custom-call(f32[3,32,2,8,384]{4,3,2,1,0:T(8,128)} %pad.4.send), custom_call_target="tpu_custom_call" | custom-call | tf_op jit(solution)/shard_map/plane_gram/pallas_call | solution.py:207
  138.2 0.9 slice_reduce_fusion.1
  139.1 1.0 slice_reduce_fusion
  140.1 1.2 reshape.120
  141.3 0.2 reshape.121
  141.6 0.8 fusion.3
  (5 shorter events, 0.0 us)
Async XLA Ops:
  0.0 4.1 %copy-start = (s32[3,352,256]{2,1,0:T(8,128)S(1)}, s32[3,352,256]{2,1,0:T(8,128)}, u32[]{:S(2)}) copy-start(s32[3,352,256]{2,1,0:T(8,128)} %param.7) | copy-start | bytes 3244036

commit v3 on v2

--- a/solution.py
+++ b/solution.py
@@ -18,7 +18,7 @@
 Z = 16
 HALF = Z // 2
 PEERS = Y * BANDS
-LAG = 3
+LAG = 7
 BLOCKS = [(b, j) for b in range(BANDS) for j in range(BAND_PAD * b // LANES, TILES)]
 PER_CYCLE = len(BLOCKS)
 PIECES = PER_CYCLE * CYCLE_DEV
@@ -66,8 +66,7 @@
 
         pltpu.make_async_copy(send.at[m, me], recv.at[m, me], own_sem.at[m]).start()
 
-    @pl.loop(0, CYCLE_DEV)
-    def _(m):
+    def partial_grams(m):
         pltpu.make_async_copy(send.at[m, me], recv.at[m, me], own_sem.at[m]).wait()
         others = recv.at[m, pl.ds(0, PEERS - 1)]
         pltpu.make_async_copy(others, others, swap_recv.at[m]).wait()
@@ -116,8 +115,7 @@
     up_lag = s * LAG
     dn_lag = jnp.where(s == 0, HALF * LAG, (HALF - 1 - s) * LAG)
 
-    @pl.loop(0, PIECES + HALF * LAG)
-    def _(step):
+    def advance(step):
         p = step - up_lag
 
         @pl.when((p >= 0) & (p < PIECES))
@@ -176,6 +174,18 @@
                     @pl.loop(1, BANDS)
                     def _(i):
                         hand_out(m, (t + i) % BANDS).start()
+
+    @pl.loop(0, CYCLE_DEV)
+    def _(m):
+        partial_grams(m)
+
+        @pl.loop(m * PER_CYCLE, (m + 1) * PER_CYCLE)
+        def _(step):
+            advance(step)
+
+    @pl.loop(PIECES, PIECES + HALF * LAG)
+    def _(step):
+        advance(step)
 
     @pl.loop(0, CYCLE_DEV)
     def _(m):

time: 143 us -> 104 us (0.73)
  Pallas kernels: 127 us -> 87.7 us
    pallas_call x1, Pallas kernels: 127 us -> 87.7 us  [summed_bands(): pl.pallas_call(kernel, out_shape=jax.ShapeDtypeStruct((CYCLE_DEV, BAND_PA...]
where the time goes in v3:
time: 104 us; the launch traced here: 103 us
  Pallas kernels  87.7 us (84%)
  local copies, waits for them, and re-layouts  9.03 us (9%)
  other arithmetic  4.23 us (4%)
  matrix products  2.27 us (2%)
    pallas_call x1, Pallas kernels, summed_bands(): pl.pallas_call(kernel, out_shape=jax.ShapeDtypeStruct((CYCLE_DEV, BAND_PA...  87.7 us
    dot_general x1, matrix products, slot_rows(): lax.dot_general(chosen, grouped, (((1,), (1,)), ((), ())), precision=lax....  2.27 us

profile of v3, /device:TPU:5, one launch (start us, length us, event | category | flops | bytes accessed | tf_op | source)
XLA Modules:
  0.0 103.3 jit_solution(13643945717387840047)
XLA Ops:
  0.0 0.0 copy-start
  0.0 0.1 pad.6.clone
  0.1 0.1 pad.7.clone
  0.2 0.9 convert_reduce_fusion
  1.0 0.8 select_reduce_fusion
  1.9 0.8 fusion.13
  2.7 0.1 iota_add_fusion
  2.8 0.1 add.100
  2.9 1.1 %slice_bitcast_fusion.2 = (bf16[352,256]{1,0:T(8,128)(2,1)S(1)}, bf16[352,256]{1,0:T(8,128)(2,1)S(1)}, bf16[352,256]{1,0:T(8,128)(2,1)S(1)}) fusion(bf16[3,352,256]{2,1,0:T(8,128)(2,1)} %param.8), kind=kLoop, calls=%fused_computation.15 | loop fusion | bytes 1081344 | tf_op jit(solution)/shard_map/squeeze | solution.py:249
  4.1 0.0 copy-done
  4.1 1.4 %select_multiply_fusion = f32[3,352,256]{2,1,0:T(8,128)S(1)} fusion(bf16[3,352,256]{2,1,0:T(8,128)(2,1)} %param.6, f32[256]{0:T(256)S(1)} %bitcast.25, f32[256]{0:T(256)S(1)} %bitcast.26, f32[256]{0:T(256)S(1)} %bitcast.24, s32[3,352,256]{2,1,0:T(8,128)S(1)} %copy-done, bf16[352,256]{1,0:T(8,128)(2,1)S(1)} %get-tuple-element.6, ...), kind=kLoop, calls=%fused_computation.1 | loop fusion | flops 2703360 | bytes 3247104 | tf_op jit(solution)/shard_map/mul | solution.py:252
  5.5 0.1 reshape.117
  5.6 0.2 maximum_maximum_fusion
  5.8 2.3 %fusion = f32[384,1152]{1,0:T(8,128)} fusion(f32[1152,256]{1,0:T(8,128)S(1)} %bitcast.19, s32[256]{0:T(256)S(1)} %multiply_add_fusion, s32[384]{0:T(512)S(1)} %add.100), kind=kOutput, calls=%fused_computation.2 | convolution fusion | flops 1359052800 | bytes 2951680 | tf_op jit(solution)/shard_map/dot_general | solution.py:266
  8.1 1.7 %reshape.119 = f32[3,32,2,6,384]{4,3,2,1,0:T(8,128)S(1)} reshape(f32[384,1152]{1,0:T(8,128)} %fusion) | data formatting | bytes 3538944 | tf_op jit(solution)/shard_map/reshape | solution.py:294
  9.8 1.6 %pad.4.send = f32[3,32,2,8,384]{4,3,2,1,0:T(8,128)} pad(f32[3,32,2,6,384]{4,3,2,1,0:T(8,128)S(1)} %reshape.119, f32[]{:T(128)} %constant.82.clone.1), padding=0_0x0_0x0_0x0_2x0_0 | pad | bytes 4128772 | tf_op jit(solution)/shard_map/jit(_pad)/pad | solution.py:295
  11.5 87.7 %plane_gram.1 = f32[3,48,384]{2,1,0:T(8,128)} custom-call(f32[3,32,2,8,384]{4,3,2,1,0:T(8,128)} %pad.4.send), custom_call_target="tpu_custom_call" | custom-call | tf_op jit(solution)/shard_map/plane_gram/pallas_call | solution.py:217
  99.1 0.9 slice_reduce_fusion.1
  100.0 1.0 %slice_reduce_fusion = f32[3,44]{1,0:T(4,128)S(1)} fusion(f32[3,48,384]{2,1,0:T(8,128)} %plane_gram.1), kind=kLoop, calls=%fused_computation.17 | loop fusion | bytes 1056 | tf_op jit(solution)/shard_map/slice | solution.py:273
  101.1 1.2 %reshape.120 = f32[3,48,8,48]{3,2,1,0:T(8,128)S(1)} reshape(f32[3,48,384]{2,1,0:T(8,128)} %plane_gram.1) | data formatting | bytes 442368 | tf_op jit(solution)/shard_map/reshape | solution.py:274
  102.2 0.2 reshape.121
  102.5 0.8 fusion.3
  (5 shorter events, 0.0 us)
Async XLA Ops:
  0.0 4.1 %copy-start = (s32[3,352,256]{2,1,0:T(8,128)S(1)}, s32[3,352,256]{2,1,0:T(8,128)}, u32[]{:S(2)}) copy-start(s32[3,352,256]{2,1,0:T(8,128)} %param.7) | copy-start | bytes 3244036

commit v4 on v3

--- a/solution.py
+++ b/solution.py
@@ -241,59 +241,84 @@
     )(send)
 
 
-def slot_rows(raw_frames, gain_section, dark_offset, rel_gain, labels, slots, cycle_slot, bands):
-    trains, pulses, pixels = raw_frames.shape
-    section_zero = gain_section == 0
-    section_one = gain_section == 1
-    offset = jnp.where(
-        section_zero, dark_offset[0], jnp.where(section_one, dark_offset[1], dark_offset[2])
-    ).astype(jnp.float32)
-    factor = jnp.where(section_zero, rel_gain[0], jnp.where(section_one, rel_gain[1], rel_gain[2]))
-    intensity = (raw_frames.astype(jnp.float32) - offset) * factor
-    band = pulses // bands
-    grouped = intensity.reshape(trains, bands, band, pixels)
-    ones = jnp.ones((trains, bands, 1, pixels), jnp.float32)
-    zeros = jnp.zeros((trains, bands, BAND_PAD - band - 1, pixels), jnp.float32)
-    grouped = jnp.concatenate([grouped, ones, zeros], axis=2).reshape(-1, pixels)
-    cycle_count = cycle_slot.shape[0]
-    member = labels[None, :] == jnp.arange(cycle_count, dtype=jnp.int32)[:, None]
-    slot_of = jnp.sum(jnp.where(member, cycle_slot[:, None], 0), axis=0)
-    index = jnp.arange(pixels, dtype=jnp.int32)
-    earlier = (labels[:, None] == labels[None, :]) & (index[:, None] < index[None, :])
-    within = jnp.sum(earlier.astype(jnp.int32), axis=0)
-    position = slot_of * DEPTH + within
-    chosen = (slots[:, None] == position[None, :]).astype(jnp.float32)
-    return lax.dot_general(
-        chosen, grouped, (((1,), (1,)), ((), ())), precision=lax.Precision.HIGHEST
+def prepare_kernel(raw, section, dark, gain, label, cycle_slot, send, banded):
+    trains, pulses, pixels = raw.shape
+    cycles = cycle_slot.shape[1]
+    band = pulses // BANDS
+    f32, bf16 = jnp.float32, jnp.bfloat16
+
+    place = lax.broadcasted_iota(jnp.int32, (cycles, cycles), 0)
+    slot = 12 * ((place >> 1) & 7) + 96 * (place & 1) + 3 * ((place >> 4) & 3) + (place >> 6)
+    cycle = lax.broadcasted_iota(jnp.int32, (cycles, cycles), 1)
+    cycle = jnp.sum(jnp.where(slot == cycle_slot[...], cycle, 0), axis=1, keepdims=True)
+    member = (cycle == label[...]).astype(f32)
+    before = lax.broadcasted_iota(jnp.int32, (pixels, pixels), 0)
+    before = (before < lax.broadcasted_iota(jnp.int32, (pixels, pixels), 1)).astype(bf16)
+    earlier = jnp.dot(member.astype(bf16), before, preferred_element_type=f32)
+    chosen = jnp.concatenate(
+        [jnp.where(earlier == w, member, 0.0).astype(bf16) for w in range(DEPTH)], 0
     )
 
-
-def normalise(total, band, bands):
-    scale = total[:, band, band]
-    rows_mean = total[:, :band, band]
-    spread = total.reshape(total.shape[0], BAND_PAD, bands, BAND_PAD)[:, :, :, :band]
-    spread = spread.reshape(total.shape[0], BAND_PAD, bands * band)
-    return (
-        scale[:, None, None]
-        * spread[:, :band]
-        / (rows_mean[:, :, None] * spread[:, band : band + 1, :])
-    )
+    edge = lax.broadcasted_iota(jnp.int32, (BAND_PAD - band, pixels), 0)
+    for b in range(BANDS):
+        banded[b * BAND_PAD + band : (b + 1) * BAND_PAD] = jnp.where(edge == 0, 1.0, 0.0)
+    for t in range(trains):
+        zero, one = section[t] == 0, section[t] == 1
+        offset = jnp.where(
+            zero, dark[0].astype(f32), jnp.where(one, dark[1].astype(f32), dark[2].astype(f32))
+        )
+        factor = jnp.where(zero, gain[0:1], jnp.where(one, gain[1:2], gain[2:3]))
+        intensity = (raw[t].astype(f32) - offset) * factor
+        for b in range(BANDS):
+            banded[b * BAND_PAD : b * BAND_PAD + band] = intensity[b * band : (b + 1) * band]
+        values = banded[...]
+        total = None
+        for _ in range(3):
+            head = values.astype(bf16)
+            values = values - head.astype(f32)
+            part = lax.dot_general(
+                chosen, head, (((1,), (1,)), ((), ())), preferred_element_type=f32
+            )
+            total = part if total is None else total + part
+        for w in range(DEPTH):
+            send[:, w * trains + t, :] = total[w * cycles : (w + 1) * cycles]
+    if ROWS > DEPTH * trains:
+        send[:, DEPTH * trains :, :] = jnp.zeros((cycles, ROWS - DEPTH * trains, TILES * LANES), f32)
+
+
+def finish_kernel(total, out):
+    band = out.shape[1]
+    for m in range(CYCLE_DEV):
+        gram = total[m]
+        ratio = gram[band : band + 1, band : band + 1] * gram
+        ratio = ratio / (gram[:, band : band + 1] * gram[band : band + 1, :])
+        for b in range(BANDS):
+            out[m, :, b * band : (b + 1) * band] = ratio[:band, b * BAND_PAD : b * BAND_PAD + band]
 
 
 def on_device(raw_frames, gain_section, dark_offset, rel_gain, cycle_label, cycle_slot):
     trains, pulses, pixels = raw_frames.shape
-    order = jnp.arange(CYCLE_DEV * Z * Y, dtype=jnp.int32)
-    m, rest = order // (PEERS * 2), order % (PEERS * 2)
-    peer, half = rest // 2, rest % 2
-    owner = (half * HALF + peer % BANDS) * Y + peer // BANDS
-    slots = (owner * CYCLE_DEV + m)[:, None] * DEPTH + jnp.arange(DEPTH, dtype=jnp.int32)[None, :]
-    rows = slot_rows(
-        raw_frames, gain_section, dark_offset, rel_gain, cycle_label[:, 0], slots.reshape(-1),
-        cycle_slot, BANDS,
+    cycles = cycle_slot.shape[0]
+    vmem = pl.BlockSpec(memory_space=pltpu.VMEM)
+    rows = pl.pallas_call(
+        prepare_kernel,
+        out_shape=jax.ShapeDtypeStruct((cycles, ROWS, TILES * LANES), jnp.float32),
+        in_specs=[vmem] * 6,
+        out_specs=vmem,
+        scratch_shapes=[pltpu.VMEM((BANDS * BAND_PAD, pixels), jnp.float32)],
+        name="prepare",
+    )(
+        raw_frames, gain_section, dark_offset, rel_gain, cycle_label.reshape(1, pixels),
+        cycle_slot.reshape(1, cycles),
     )
-    rows = rows.reshape(CYCLE_DEV, PEERS, 2, DEPTH * trains, TILES * LANES)
-    rows = jnp.pad(rows, ((0, 0), (0, 0), (0, 0), (0, ROWS - DEPTH * trains), (0, 0)))
-    return normalise(summed_bands(rows), pulses // BANDS, BANDS)
+    rows = rows.reshape(CYCLE_DEV, PEERS, 2, ROWS, TILES * LANES)
+    return pl.pallas_call(
+        finish_kernel,
+        out_shape=jax.ShapeDtypeStruct((CYCLE_DEV, pulses // BANDS, pulses), jnp.float32),
+        in_specs=[vmem],
+        out_specs=vmem,
+        name="finish",
+    )(summed_bands(rows))
 
 
 def solution(mesh):

time: 104 us -> 94.7 us (0.911)
  local copies, waits for them, and re-layouts: 9.03 us -> 0 us
  Pallas kernels: 87.7 us -> 94.5 us
  other arithmetic: 4.23 us -> 0 us
  matrix products: 2.27 us -> 0 us
    pallas_call x0 -> x2, Pallas kernels: none -> 6.94 us  [the longest x1 4.91 us: on_device(): pl.pallas_call(prepare_kernel, out_shape=jax.ShapeDtypeStruct((cycles, RO...]
    reshape x4 -> x0, local copies, waits for them, and re-layouts: 3.22 us -> none  [the longest x1 1.74 us: on_device(): rows = rows.reshape(CYCLE_DEV, PEERS, 2, DEPTH * trains, TILES * LANES)]
    slice x4 -> x0, local copies, waits for them, and re-layouts: 2.76 us -> none  [the longest x1 1.05 us: normalise(): rows_mean = total[:, :band, band]]
    dot_general x1 -> x0, matrix products: 2.27 us -> none  [slot_rows(): lax.dot_general(chosen, grouped, (((1,), (1,)), ((), ())), precision=lax....]
    reduce_sum x2 -> x0, other arithmetic: 1.69 us -> none  [the longest x1 0.89 us: slot_rows(): within = jnp.sum(earlier.astype(jnp.int32), axis=0)]
    pad x1 -> x0, local copies, waits for them, and re-layouts: 1.62 us -> none  [on_device(): jnp.pad(rows, ((0, 0), (0, 0), (0, 0), (0, ROWS - DEPTH * trains), (0, 0)))]
    mul x2 -> x0, other arithmetic: 1.44 us -> none  [the longest x1 1.42 us: slot_rows(): intensity = (raw_frames.astype(jnp.float32) - offset) * factor]
    squeeze x1 -> x0, local copies, waits for them, and re-layouts: 1.13 us -> none  [slot_rows(): dark_offset[0]]
where the time goes in v4:
time: 94.7 us; the launch traced here: 94.5 us
  Pallas kernels  94.5 us (100%)
    pallas_call x1, Pallas kernels, summed_bands(): pl.pallas_call(kernel, out_shape=jax.ShapeDtypeStruct((CYCLE_DEV, BAND_PA...  87.6 us
    pallas_call x1, Pallas kernels, on_device(): pl.pallas_call(prepare_kernel, out_shape=jax.ShapeDtypeStruct((cycles, RO...  4.91 us
    pallas_call x1, Pallas kernels, on_device(): pl.pallas_call(finish_kernel, out_shape=jax.ShapeDtypeStruct((CYCLE_DEV,...  2.03 us

profile of v4, /device:TPU:5, one launch (start us, length us, event | category | flops | bytes accessed | tf_op | source)
XLA Modules:
  0.0 94.5 jit_solution(4029551074841915532)
XLA Ops:
  0.0 4.9 %prepare.1 = f32[192,8,384]{2,1,0:T(8,128)} custom-call(bf16[3,352,256]{2,1,0:T(8,128)(2,1)} %raw.1, s32[3,352,256]{2,1,0:T(8,128)} %section.1, bf16[3,352,256]{2,1,0:T(8,128)(2,1)} %dark.1, f32[3,256]{1,0:T(4,128)} %gain.1, s32[1,256]{1,0:T(1,128)} %bitcast.4, s32[1,192]{1,0:T(1,128)} %bitcast.5), custom_call_target="tpu_custom_call" | custom-call | tf_op jit(solution)/shard_map/prepare/pallas_call | solution.py:303
  4.9 87.6 %plane_gram.1.total = f32[3,48,384]{2,1,0:T(8,128)} custom-call(f32[3,32,2,8,384]{4,3,2,1,0:T(8,128)} %bitcast.3), custom_call_target="tpu_custom_call" | custom-call | tf_op jit(solution)/shard_map/plane_gram/pallas_call | solution.py:217
  92.5 2.0 %finish.1 = f32[3,44,352]{2,1,0:T(8,128)} custom-call(f32[3,48,384]{2,1,0:T(8,128)} %plane_gram.1.total), custom_call_target="tpu_custom_call" | custom-call | tf_op jit(solution)/shard_map/finish/pallas_call | solution.py:315

commit v5 on v4

--- a/solution.py
+++ b/solution.py
@@ -14,6 +14,8 @@
 TILES = 3
 BANDS = 8
 ROWS = 8
+SERIES = 6
+PACKED = 40
 Y = 4
 Z = 16
 HALF = Z // 2
@@ -71,7 +73,13 @@
         others = recv.at[m, pl.ds(0, PEERS - 1)]
         pltpu.make_async_copy(others, others, swap_recv.at[m]).wait()
         for h in range(2):
-            rows = recv[m, :, h].reshape(PEERS * ROWS, TILES * LANES)
+            blank = jnp.zeros((PEERS, ROWS - SERIES, LANES), jnp.float32)
+            rows = []
+            for j in range(TILES):
+                first = (2 * j + h) * SERIES
+                tile = jnp.concatenate([recv[m, :, first : first + SERIES], blank], 1)
+                rows.append(tile.reshape(PEERS * ROWS, LANES))
+            rows = jnp.concatenate(rows, 1)
             head = rows.astype(jnp.bfloat16)
             tail = (rows - head.astype(jnp.float32)).astype(jnp.bfloat16)
             turned = rows.T
@@ -220,7 +228,7 @@
         in_specs=[pl.BlockSpec(memory_space=pltpu.VMEM)],
         out_specs=pl.BlockSpec(memory_space=pltpu.VMEM),
         scratch_shapes=[
-            pltpu.VMEM((CYCLE_DEV, PEERS, 2, ROWS, TILES * LANES), jnp.float32),
+            pltpu.VMEM((CYCLE_DEV, PEERS, PACKED, LANES), jnp.float32),
             pltpu.VMEM((2, PIECES) + piece, jnp.float32),
             pltpu.VMEM((PIECES,) + piece, jnp.float32),
             pltpu.VMEM((PIECES,) + piece, jnp.float32),
@@ -248,7 +256,9 @@
     f32, bf16 = jnp.float32, jnp.bfloat16
 
     place = lax.broadcasted_iota(jnp.int32, (cycles, cycles), 0)
-    slot = 12 * ((place >> 1) & 7) + 96 * (place & 1) + 3 * ((place >> 4) & 3) + (place >> 6)
+    half = (place >= cycles // 2).astype(jnp.int32)
+    place = place - half * (cycles // 2)
+    slot = 12 * (place & 7) + 96 * half + 3 * ((place >> 3) & 3) + (place >> 5)
     cycle = lax.broadcasted_iota(jnp.int32, (cycles, cycles), 1)
     cycle = jnp.sum(jnp.where(slot == cycle_slot[...], cycle, 0), axis=1, keepdims=True)
     member = (cycle == label[...]).astype(f32)
@@ -281,9 +291,14 @@
             )
             total = part if total is None else total + part
         for w in range(DEPTH):
-            send[:, w * trains + t, :] = total[w * cycles : (w + 1) * cycles]
-    if ROWS > DEPTH * trains:
-        send[:, DEPTH * trains :, :] = jnp.zeros((cycles, ROWS - DEPTH * trains, TILES * LANES), f32)
+            for h in range(2):
+                low = w * cycles + h * (cycles // 2)
+                for j in range(TILES):
+                    send[:, (2 * j + h) * SERIES + w * trains + t, :] = total[
+                        low : low + cycles // 2, j * LANES : (j + 1) * LANES
+                    ]
+    used = 2 * TILES * SERIES
+    send[:, used:, :] = jnp.zeros((cycles // 2, PACKED - used, LANES), f32)
 
 
 def finish_kernel(total, out):
@@ -302,7 +317,7 @@
     vmem = pl.BlockSpec(memory_space=pltpu.VMEM)
     rows = pl.pallas_call(
         prepare_kernel,
-        out_shape=jax.ShapeDtypeStruct((cycles, ROWS, TILES * LANES), jnp.float32),
+        out_shape=jax.ShapeDtypeStruct((cycles // 2, PACKED, LANES), jnp.float32),
         in_specs=[vmem] * 6,
         out_specs=vmem,
         scratch_shapes=[pltpu.VMEM((BANDS * BAND_PAD, pixels), jnp.float32)],
@@ -311,7 +326,7 @@
         raw_frames, gain_section, dark_offset, rel_gain, cycle_label.reshape(1, pixels),
         cycle_slot.reshape(1, cycles),
     )
-    rows = rows.reshape(CYCLE_DEV, PEERS, 2, ROWS, TILES * LANES)
+    rows = rows.reshape(CYCLE_DEV, PEERS, PACKED, LANES)
     return pl.pallas_call(
         finish_kernel,
         out_shape=jax.ShapeDtypeStruct((CYCLE_DEV, pulses // BANDS, pulses), jnp.float32),

time: 94.7 us -> 92.2 us (0.974)
  the two profiles are of different devices: /device:TPU:5 before, /device:TPU:65 now
where the time goes in v5:
time: 92.2 us; the launch traced here: 92 us
  Pallas kernels  91.9 us (100%)
    pallas_call x1, Pallas kernels, summed_bands(): pl.pallas_call(kernel, out_shape=jax.ShapeDtypeStruct((CYCLE_DEV, BAND_PA...  84.9 us
    pallas_call x1, Pallas kernels, on_device(): pl.pallas_call(prepare_kernel, out_shape=jax.ShapeDtypeStruct((cycles //...  5.05 us
    pallas_call x1, Pallas kernels, on_device(): pl.pallas_call(finish_kernel, out_shape=jax.ShapeDtypeStruct((CYCLE_DEV,...  2.03 us

profile of v5, /device:TPU:65, one launch (start us, length us, event | category | flops | bytes accessed | tf_op | source)
XLA Modules:
  0.0 92.0 jit_solution(6300877740998440909)
XLA Ops:
  0.0 5.1 %prepare.1 = f32[96,40,128]{2,1,0:T(8,128)} custom-call(bf16[3,352,256]{2,1,0:T(8,128)(2,1)} %raw.1, s32[3,352,256]{2,1,0:T(8,128)} %section.1, bf16[3,352,256]{2,1,0:T(8,128)(2,1)} %dark.1, f32[3,256]{1,0:T(4,128)} %gain.1, s32[1,256]{1,0:T(1,128)} %bitcast.4, s32[1,192]{1,0:T(1,128)} %bitcast.5), custom_call_target="tpu_custom_call" | custom-call | tf_op jit(solution)/shard_map/prepare/pallas_call | solution.py:318
  5.1 84.9 %plane_gram.1.total = f32[3,48,384]{2,1,0:T(8,128)} custom-call(f32[3,32,40,128]{3,2,1,0:T(8,128)} %bitcast.3), custom_call_target="tpu_custom_call" | custom-call | tf_op jit(solution)/shard_map/plane_gram/pallas_call | solution.py:225
  89.9 2.0 %finish.1 = f32[3,44,352]{2,1,0:T(8,128)} custom-call(f32[3,48,384]{2,1,0:T(8,128)} %plane_gram.1.total), custom_call_target="tpu_custom_call" | custom-call | tf_op jit(solution)/shard_map/finish/pallas_call | solution.py:330

commit v6 on v5

--- a/solution.py
+++ b/solution.py
@@ -20,9 +20,10 @@
 Z = 16
 HALF = Z // 2
 PEERS = Y * BANDS
-LAG = 7
+LAG = 13
 BLOCKS = [(b, j) for b in range(BANDS) for j in range(BAND_PAD * b // LANES, TILES)]
-PER_CYCLE = len(BLOCKS)
+PER_CYCLE = 2 * len(BLOCKS)
+PIECE_ROWS = BAND_PAD // 2
 PIECES = PER_CYCLE * CYCLE_DEV
 MESH = pl.DeviceIdType.MESH
 
@@ -97,10 +98,11 @@
                 )
                 for b in bands:
                     for jj in range(j, TILES):
-                        gram[h, m * PER_CYCLE + BLOCKS.index((b, jj))] = part[
-                            b * BAND_PAD - low : (b + 1) * BAND_PAD - low,
-                            (jj - j) * LANES : (jj - j + 1) * LANES,
-                        ]
+                        for e in range(2):
+                            top = b * BAND_PAD - low + e * PIECE_ROWS
+                            gram[h, m * PER_CYCLE + 2 * BLOCKS.index((b, jj)) + e] = part[
+                                top : top + PIECE_ROWS, (jj - j) * LANES : (jj - j + 1) * LANES
+                            ]
 
     def up_copy(p):
         return pltpu.make_async_remote_copy(
@@ -159,7 +161,8 @@
                     m = q // PER_CYCLE
 
                     def block(b, j):
-                        return gram[near, m * PER_CYCLE + BLOCKS.index((b, j))]
+                        first = m * PER_CYCLE + 2 * BLOCKS.index((b, j))
+                        return jnp.concatenate([gram[near, first], gram[near, first + 1]], 0)
 
                     for b, j in BLOCKS:
                         full[m, b, j] = block(b, j)
@@ -229,9 +232,9 @@
         out_specs=pl.BlockSpec(memory_space=pltpu.VMEM),
         scratch_shapes=[
             pltpu.VMEM((CYCLE_DEV, PEERS, PACKED, LANES), jnp.float32),
-            pltpu.VMEM((2, PIECES) + piece, jnp.float32),
-            pltpu.VMEM((PIECES,) + piece, jnp.float32),
-            pltpu.VMEM((PIECES,) + piece, jnp.float32),
+            pltpu.VMEM((2, PIECES, PIECE_ROWS, LANES), jnp.float32),
+            pltpu.VMEM((PIECES, PIECE_ROWS, LANES), jnp.float32),
+            pltpu.VMEM((PIECES, PIECE_ROWS, LANES), jnp.float32),
             pltpu.VMEM((CYCLE_DEV, BANDS, TILES) + piece, jnp.float32),
             pltpu.VMEM((CYCLE_DEV, TILES) + piece, jnp.float32),
             pltpu.SemaphoreType.DMA((CYCLE_DEV,)),

time: 92.2 us -> 92 us (level)
  no operation moved by 1% of the time
where the time goes in v6:
time: 92 us; the launch traced here: 91.8 us
  Pallas kernels  91.8 us (100%)
    pallas_call x1, Pallas kernels, summed_bands(): pl.pallas_call(kernel, out_shape=jax.ShapeDtypeStruct((CYCLE_DEV, BAND_PA...  84.7 us
    pallas_call x1, Pallas kernels, on_device(): pl.pallas_call(prepare_kernel, out_shape=jax.ShapeDtypeStruct((cycles //...  5.05 us
    pallas_call x1, Pallas kernels, on_device(): pl.pallas_call(finish_kernel, out_shape=jax.ShapeDtypeStruct((CYCLE_DEV,...  2.03 us

profile of v6, /device:TPU:65, one launch (start us, length us, event | category | flops | bytes accessed | tf_op | source)
XLA Modules:
  0.0 91.8 jit_solution(1686744561166495230)
XLA Ops:
  0.0 5.1 %prepare.1 = f32[96,40,128]{2,1,0:T(8,128)} custom-call(bf16[3,352,256]{2,1,0:T(8,128)(2,1)} %raw.1, s32[3,352,256]{2,1,0:T(8,128)} %section.1, bf16[3,352,256]{2,1,0:T(8,128)(2,1)} %dark.1, f32[3,256]{1,0:T(4,128)} %gain.1, s32[1,256]{1,0:T(1,128)} %bitcast.4, s32[1,192]{1,0:T(1,128)} %bitcast.5), custom_call_target="tpu_custom_call" | custom-call | tf_op jit(solution)/shard_map/prepare/pallas_call | solution.py:321
  5.1 84.7 %plane_gram.1.total = f32[3,48,384]{2,1,0:T(8,128)} custom-call(f32[3,32,40,128]{3,2,1,0:T(8,128)} %bitcast.3), custom_call_target="tpu_custom_call" | custom-call | tf_op jit(solution)/shard_map/plane_gram/pallas_call | solution.py:228
  89.8 2.0 %finish.1 = f32[3,44,352]{2,1,0:T(8,128)} custom-call(f32[3,48,384]{2,1,0:T(8,128)} %plane_gram.1.total), custom_call_target="tpu_custom_call" | custom-call | tf_op jit(solution)/shard_map/finish/pallas_call | solution.py:333
